TPU v7x, 32 devices: a whole 2x2x4 slice. The times are simulated.
32 devices in a mesh: ctx: 8 (over y, x, core), wa: 4 (over z).
Axes of the slice: x: 2, y: 2, z: 4, core: 2. Of those that a mesh axis runs over, the one named last changes fastest.
Arguments:
- tokens: bfloat16 [4, 1024, 2048], P('wa', 'ctx'), may hold values from -6 to 6
- lengths: int32 [4, 2], P('wa'), may hold values from 384 to 640, as said below
- dealing: int32 [4, 8], P('wa'), may hold values from 0 to 7, each once within a row
- norm1_gain: float32 [2048], replicated, may hold values from 0.1 to 1.9
- w_qkv: bfloat16 [2048, 6144], P('wa'), may hold values from -0.125 to 0.125
- w_out: bfloat16 [2048, 2048], P('wa'), may hold values from -2 to 2
- norm2_gain: float32 [2048], replicated, may hold values from 0.1 to 1.9
- w_gate_up: bfloat16 [2048, 11008], P('wa'), may hold values from -0.125 to 0.125
- w_down: bfloat16 [5504, 2048], P('wa'), may hold values from -0.078125 to 0.078125
- grad_out: bfloat16 [4, 1024, 2048], P('wa', 'ctx'), may hold values from -6 to 6
Outputs:
- out: bfloat16 [4, 1024, 2048], P('wa', 'ctx')
- d_tokens: bfloat16 [4, 1024, 2048], P('wa', 'ctx')
- d_norm1_gain: float32 [2048], replicated
- d_w_qkv: float32 [2048, 6144], P('wa')
- d_w_out: float32 [2048, 2048], P('wa')
- d_norm2_gain: float32 [2048], replicated
- d_w_gate_up: float32 [2048, 11008], P('wa')
- d_w_down: float32 [5504, 2048], P('wa')
Inputs may be any that keep to these rules, and one draw needn't show every extreme that they name: Each row holds the lengths of the two sequences of that group, first sequence first; they sum to 1024; some row holds a sequence of exactly 384 tokens. `dealing`: each row is a permutation of the block numbers of the group.
All inputs are finite; a program needn't handle non-finite values.
Results may differ from a plain program's by a relative error of at most 0.019.
Values may be sent and summed in bfloat16 or wider, within the bound.
A program may use at most 576 MiB of HBM per device.

v0:
```python
import math
import jax
import jax.numpy as jnp
from jax import lax
from jax.sharding import PartitionSpec as P

HEADS = 16
HEAD = 128
FF = 5504
WINDOW = 2048
BLOCK = 128
EPSILON = 1e-06


def dot_plain(left, right):
    return jnp.dot(left, right, preferred_element_type=jnp.float32)


def dot_right_t(left, right):
    return lax.dot_general(
        left, right, (((1,), (1,)), ((), ())), preferred_element_type=jnp.float32
    )


def dot_left_t(left, right):
    return lax.dot_general(
        left, right, (((0,), (0,)), ((), ())), preferred_element_type=jnp.float32
    )


def rms_scale(values):
    return lax.rsqrt(jnp.mean(values * values, axis=-1, keepdims=True) + EPSILON)


def rotary_tables(seq_pos):
    half_width = HEAD // 2
    inverse_freq = jnp.power(10000.0, -2.0 * jnp.arange(half_width, dtype=jnp.float32) / HEAD)
    angles = seq_pos.astype(jnp.float32)[:, None] * inverse_freq[None, :]
    return (jnp.cos(angles)[:, None, :], jnp.sin(angles)[:, None, :])


def rotate(values, cosine, sine):
    half_width = HEAD // 2
    first_half = values[..., :half_width]
    second_half = values[..., half_width:]
    return jnp.concatenate(
        [first_half * cosine - second_half * sine, first_half * sine + second_half * cosine],
        axis=-1,
    )


def unrotate(values, cosine, sine):
    half_width = HEAD // 2
    first_half = values[..., :half_width]
    second_half = values[..., half_width:]
    return jnp.concatenate(
        [first_half * cosine + second_half * sine, second_half * cosine - first_half * sine],
        axis=-1,
    )


def row_picker(targets, carried, segment):
    inside = (targets >= 0) & (targets < segment.shape[0])
    taken_rows = jnp.take(segment, jnp.clip(targets, 0, segment.shape[0] - 1), axis=0)
    return jnp.where(inside[:, None], taken_rows, carried)


def per_device(
    tokens, lengths, dealing, norm1_gain, w_qkv, w_out, norm2_gain, w_gate_up, w_down, grad_out
):
    tok_rows = tokens.shape[1]
    width = tokens.shape[2]
    ctx_index = lax.axis_index("ctx")
    block_order = dealing[0]
    block_total = block_order.shape[0]
    group_rows = block_total * BLOCK
    own_blocks = tok_rows // BLOCK
    first_length = lengths[0, 0]
    in_block = jnp.arange(BLOCK, dtype=jnp.int32)
    key_pos = jnp.repeat(block_order, BLOCK) * BLOCK + jnp.tile(in_block, block_total)
    key_seg = (key_pos >= first_length).astype(jnp.int32)
    query_pos = lax.dynamic_slice_in_dim(key_pos, ctx_index * tok_rows, tok_rows)
    query_seg = lax.dynamic_slice_in_dim(key_seg, ctx_index * tok_rows, tok_rows)
    cosine, sine = rotary_tables(query_pos - query_seg * first_length)
    distance = query_pos[:, None] - key_pos[None, :]
    allowed = (query_seg[:, None] == key_seg[None, :]) & (distance >= 0) & (distance < WINDOW)
    block_ids = jnp.arange(block_total, dtype=jnp.int32)
    inverse = jnp.sum(
        jnp.where(block_order[None, :] == block_ids[:, None], block_ids[None, :], 0), axis=1
    )
    own_sources = lax.dynamic_slice_in_dim(inverse, ctx_index * own_blocks, own_blocks)
    source_rows = jnp.repeat(own_sources, BLOCK) * BLOCK + jnp.tile(in_block, own_blocks)
    empty_rows = jnp.zeros((tok_rows, width), jnp.bfloat16)
    cotangent = row_picker(
        query_pos, empty_rows, lax.all_gather(grad_out[0], "ctx", axis=0, tiled=True)
    )
    inputs = tokens[0].astype(jnp.float32)
    scale_one = rms_scale(inputs)
    normed_one = inputs * scale_one
    act_one = (normed_one * norm1_gain).astype(jnp.bfloat16)
    full_qkv, full_out = (
        lax.all_gather(w_qkv, "wa", axis=0, tiled=True),
        lax.all_gather(w_out, "wa", axis=0, tiled=True),
    )
    projected = dot_plain(act_one, full_qkv)
    query_b = rotate(projected[:, :width].reshape(tok_rows, HEADS, HEAD), cosine, sine).astype(
        jnp.bfloat16
    )
    key_b = rotate(
        projected[:, width : 2 * width].reshape(tok_rows, HEADS, HEAD), cosine, sine
    ).astype(jnp.bfloat16)
    value_b = projected[:, 2 * width :].astype(jnp.bfloat16)
    kv_local = jnp.concatenate([key_b.reshape(tok_rows, width), value_b], axis=1)
    kv_all = lax.all_gather(kv_local, "ctx", axis=0, tiled=True)
    keys_all = kv_all[:, :width].reshape(group_rows, HEADS, HEAD)
    values_all = kv_all[:, width:].reshape(group_rows, HEADS, HEAD)
    score_scale = math.sqrt(HEAD)
    per_group = min(4, HEADS)
    mixed_parts = []
    total_parts = []
    for head_first in range(0, HEADS, per_group):
        query_part = query_b[:, head_first : head_first + per_group]
        key_part = keys_all[:, head_first : head_first + per_group]
        value_part = values_all[:, head_first : head_first + per_group]
        scores = (
            jnp.einsum("qhe,khe->hqk", query_part, key_part, preferred_element_type=jnp.float32)
            / score_scale
        )
        scores = jnp.where(allowed[None], scores, -jnp.inf)
        largest = jnp.max(scores, axis=2, keepdims=True)
        log_total = largest + jnp.log(jnp.sum(jnp.exp(scores - largest), axis=2, keepdims=True))
        probs_b = jnp.exp(scores - log_total).astype(jnp.bfloat16)
        mixed_parts.append(
            jnp.einsum("hqk,khe->qhe", probs_b, value_part, preferred_element_type=jnp.float32)
        )
        total_parts.append(log_total[:, :, 0])
    log_totals = jnp.concatenate(total_parts, axis=0)
    attended_b = jnp.concatenate(mixed_parts, axis=1).reshape(tok_rows, width).astype(jnp.bfloat16)
    hidden = inputs + dot_plain(attended_b, full_out)
    scale_two = rms_scale(hidden)
    normed_two = hidden * scale_two
    act_two = (normed_two * norm2_gain).astype(jnp.bfloat16)
    full_gate_up, full_down = (
        lax.all_gather(w_gate_up, "wa", axis=0, tiled=True),
        lax.all_gather(w_down, "wa", axis=0, tiled=True),
    )
    gate_up = dot_plain(act_two, full_gate_up)
    gate_part = gate_up[:, :FF]
    up_part = gate_up[:, FF:]
    sigmoid_gate = jax.nn.sigmoid(gate_part)
    silu_gate = gate_part * sigmoid_gate
    inner_b = (silu_gate * up_part).astype(jnp.bfloat16)
    result_b = (hidden + dot_plain(inner_b, full_down)).astype(jnp.bfloat16)
    out_given = row_picker(
        source_rows, empty_rows, lax.all_gather(result_b, "ctx", axis=0, tiled=True)
    )
    back_gate_up, back_down = (
        lax.all_gather(w_gate_up, "wa", axis=0, tiled=True),
        lax.all_gather(w_down, "wa", axis=0, tiled=True),
    )
    down_share = lax.psum_scatter(
        dot_left_t(inner_b, cotangent).astype(jnp.bfloat16), "wa", scatter_dimension=0, tiled=True
    )
    d_inner = dot_right_t(cotangent, back_down)
    d_gate = d_inner * up_part * sigmoid_gate * (1.0 + gate_part * (1.0 - sigmoid_gate))
    d_gate_up_b = jnp.concatenate([d_gate, d_inner * silu_gate], axis=1).astype(jnp.bfloat16)
    gate_up_share = lax.psum_scatter(
        dot_left_t(act_two, d_gate_up_b).astype(jnp.bfloat16), "wa", scatter_dimension=0, tiled=True
    )
    d_normed_two = dot_right_t(d_gate_up_b, back_gate_up)
    gain_two_part = jnp.sum(d_normed_two * normed_two, axis=0)
    scaled_two = d_normed_two * norm2_gain
    d_hidden = cotangent.astype(jnp.float32) + scale_two * (
        scaled_two - normed_two * jnp.mean(scaled_two * normed_two, axis=1, keepdims=True)
    )
    d_branch_b = d_hidden.astype(jnp.bfloat16)
    back_qkv, back_out = (
        lax.all_gather(w_qkv, "wa", axis=0, tiled=True),
        lax.all_gather(w_out, "wa", axis=0, tiled=True),
    )
    grad_mixed_b = (
        dot_right_t(d_branch_b, back_out).astype(jnp.bfloat16).reshape(tok_rows, HEADS, HEAD)
    )
    head_steps = HEADS // per_group

    def make_backward():

        def backward_heads(head_index, carried):
            d_query, d_keys_values, row_dots = carried
            head_first = head_index * per_group
            query_part = lax.dynamic_slice_in_dim(query_b, head_first, per_group, 1)
            key_part = lax.dynamic_slice_in_dim(keys_all, head_first, per_group, 1)
            value_part = lax.dynamic_slice_in_dim(values_all, head_first, per_group, 1)
            grad_part = lax.dynamic_slice_in_dim(grad_mixed_b, head_first, per_group, 1)
            log_part = lax.dynamic_slice_in_dim(log_totals, head_first, per_group, 0)
            scores = (
                jnp.einsum("qhe,khe->hqk", query_part, key_part, preferred_element_type=jnp.float32)
                / score_scale
            )
            scores = jnp.where(allowed[None], scores, -jnp.inf)
            probs = jnp.exp(scores - log_part[:, :, None])
            d_probs = jnp.einsum(
                "qhe,khe->hqk", grad_part, value_part, preferred_element_type=jnp.float32
            )
            row_dot = jnp.sum(probs * d_probs, axis=2)
            d_scores = (probs * (d_probs - row_dot[:, :, None])).astype(jnp.bfloat16)
            query_grad = (
                jnp.einsum("hqk,khe->qhe", d_scores, key_part, preferred_element_type=jnp.float32)
                / score_scale
            )
            d_query = lax.dynamic_update_slice_in_dim(d_query, query_grad, head_first, 1)
            row_dots = lax.dynamic_update_slice_in_dim(row_dots, row_dot, head_first, 0)
            key_grad = (
                jnp.einsum("hqk,qhe->khe", d_scores, query_part, preferred_element_type=jnp.float32)
                / score_scale
            )
            value_grad = jnp.einsum(
                "hqk,qhe->khe",
                probs.astype(jnp.bfloat16),
                grad_part,
                preferred_element_type=jnp.float32,
            )
            d_keys_values = lax.dynamic_update_slice_in_dim(
                d_keys_values, key_grad.reshape(group_rows, per_group * HEAD), head_first * HEAD, 1
            )
            d_keys_values = lax.dynamic_update_slice_in_dim(
                d_keys_values,
                value_grad.reshape(group_rows, per_group * HEAD),
                width + head_first * HEAD,
                1,
            )
            return (d_query, d_keys_values, row_dots)

        return backward_heads

    start_query = jnp.zeros((tok_rows, HEADS, HEAD), jnp.float32)
    start_dots = jnp.zeros((HEADS, tok_rows), jnp.float32)
    start_keys_values = jnp.zeros((group_rows, 2 * width), jnp.float32)
    d_query, d_keys_values, row_dots = lax.fori_loop(
        0, head_steps, make_backward(), (start_query, start_keys_values, start_dots)
    )
    d_kv_mine = lax.psum_scatter(d_keys_values, "ctx", scatter_dimension=0, tiled=True)
    key_rot_grad = d_kv_mine[:, :width].reshape(tok_rows, HEADS, HEAD)
    d_qkv_b = jnp.concatenate(
        [
            unrotate(d_query, cosine, sine).reshape(tok_rows, width),
            unrotate(key_rot_grad, cosine, sine).reshape(tok_rows, width),
            d_kv_mine[:, width:],
        ],
        axis=1,
    ).astype(jnp.bfloat16)
    qkv_part = dot_left_t(act_one, d_qkv_b)
    out_part = dot_left_t(attended_b, d_branch_b)
    attn_share = lax.psum_scatter(
        jnp.concatenate([qkv_part, out_part], axis=1).astype(jnp.bfloat16),
        "wa",
        scatter_dimension=0,
        tiled=True,
    )
    d_normed_one = dot_right_t(d_qkv_b, back_qkv)
    gain_one_part = jnp.sum(d_normed_one * normed_one, axis=0)
    scaled_one = d_normed_one * norm1_gain
    d_inputs = d_hidden + scale_one * (
        scaled_one - normed_one * jnp.mean(scaled_one * normed_one, axis=1, keepdims=True)
    )
    gain_one_sum, gain_two_sum = lax.psum((gain_one_part, gain_two_part), ("ctx", "wa"))
    attn_total, gate_up_total, down_total = (
        lax.psum(attn_share, "ctx").astype(jnp.float32),
        lax.psum(gate_up_share, "ctx").astype(jnp.float32),
        lax.psum(down_share, "ctx").astype(jnp.float32),
    )
    return (
        out_given[None],
        d_inputs.astype(jnp.bfloat16)[None],
        gain_one_sum,
        attn_total[:, : 3 * width],
        attn_total[:, 3 * width :],
        gain_two_sum,
        gate_up_total,
        down_total,
    )


def solution(mesh):
    in_specs = (
        P("wa", "ctx", None),
        P("wa", None),
        P("wa", None),
        P(),
        P("wa", None),
        P("wa", None),
        P(),
        P("wa", None),
        P("wa", None),
        P("wa", "ctx", None),
    )
    out_specs = (
        P("wa", "ctx", None),
        P("wa", "ctx", None),
        P(),
        P("wa", None),
        P("wa", None),
        P(),
        P("wa", None),
        P("wa", None),
    )
    return jax.shard_map(
        per_device, mesh=mesh, in_specs=in_specs, out_specs=out_specs, check_vma=False
    )
```

profile of v0, /device:TPU:0, one launch (start us, length us, event | category | flops | bytes accessed | tf_op | source)
XLA Modules:
  0.0 4124.8 jit_solution(4794331274431847272)
XLA Ops:
  9.7 427.8 %all-gather.9.cloned.1.call-done = bf16[2048,6144]{1,0:T(8,128)(2,1)} async-done(((bf16[512,6144]{1,0:T(8,128)(2,1)}), bf16[2048,6144]{1,0:T(8,128)(2,1)}) %all-gather.9.cloned.1.call-update) | async-done | bytes 25165840 | tf_op jit(solution)/shard_map/all_gather | solution.py:102
  437.5 10.5 fusion.58
  454.2 20.2 all-gather.21.cloned.1.call-done
  474.4 4.2 gather_fusion.1
  478.9 52.4 %all-gather.11.cloned.1.call-done = bf16[1024,4096]{1,0:T(8,128)(2,1)} async-done(((bf16[128,4096]{1,0:T(8,128)(2,1)}), bf16[1024,4096]{1,0:T(8,128)(2,1)}) %all-gather.11.cloned.1.call-update) | async-done | bytes 8388624 | tf_op jit(solution)/shard_map/all_gather | solution.py:114
  531.3 4.0 slice_bitcast_fusion.1
  546.7 135.7 %all-gather.13.cloned.1.call-done = bf16[2048,2048]{1,0:T(8,128)(2,1)} async-done(((bf16[512,2048]{1,0:T(8,128)(2,1)}), bf16[2048,2048]{1,0:T(8,128)(2,1)}) %all-gather.13.cloned.1.call-update) | async-done | bytes 8388624 | tf_op jit(solution)/shard_map/all_gather | solution.py:103
  682.4 4.8 multiply_reduce_fusion.3
  687.1 745.7 %all-gather.15.cloned.1.call-done = bf16[2048,11008]{1,0:T(8,128)(2,1)} async-done(((bf16[512,11008]{1,0:T(8,128)(2,1)}), bf16[2048,11008]{1,0:T(8,128)(2,1)}) %all-gather.15.cloned.1.call-update) | async-done | bytes 45088784 | tf_op jit(solution)/shard_map/all_gather | solution.py:144
  1432.8 24.1 fusion.64
  1456.9 358.1 %all-gather.17.cloned.1.call-done = bf16[5504,2048]{1,0:T(8,128)(2,1)} async-done(((bf16[1376,2048]{1,0:T(8,128)(2,1)}), bf16[5504,2048]{1,0:T(8,128)(2,1)}) %all-gather.17.cloned.1.call-update) | async-done | bytes 22544400 | tf_op jit(solution)/shard_map/all_gather | solution.py:145
  1815.0 14.9 multiply_convert_fusion.2
  1829.9 21.4 multiply_reduce_fusion.1
  1851.8 6.7 fusion.25
  1859.7 7.9 broadcast_in_dim.154
  1867.6 75.1 %while.18 = (s32[]{:T(128)}, f32[128,16,128]{2,0,1:T(8,128)}, f32[1024,4096]{0,1:T(8,128)}, bf16[1024,16,128]{2,0,1:T(8,128)(2,1)}, bf16[128,16,128]{2,0,1:T(8,1...) while((s32[]{:T(128)}, f32[128,16,128]{2,0,1:T(8,128)}, ...), condition=%wide.region_14.16_spmd.clone, body=%wide.region_12.15_spmd.clone.sunk | while | flops 677182976 | bytes 61174424 | solution.py:239
  1867.8 2.5 constant_dynamic-slice_fusion.6
  1873.8 1.7 constant_dynamic-update-slice_fusion.6
  1875.5 2.7 convolution_multiply_fusion.3
  1878.2 3.1 constant_dynamic-update-slice_fusion.7
  1881.3 1.8 fusion.115
  1883.2 3.3 constant_dynamic-update-slice_fusion.8
  1886.6 2.5 constant_dynamic-slice_fusion.6
  1894.3 2.7 convolution_multiply_fusion.3
  1897.0 3.2 constant_dynamic-update-slice_fusion.7
  1900.2 1.8 fusion.115
  1902.0 3.2 constant_dynamic-update-slice_fusion.8
  1905.3 2.5 constant_dynamic-slice_fusion.6
  1913.0 2.7 convolution_multiply_fusion.3
  1915.7 3.2 constant_dynamic-update-slice_fusion.7
  1918.9 1.8 fusion.115
  1920.7 3.2 constant_dynamic-update-slice_fusion.8
  1924.1 2.5 constant_dynamic-slice_fusion.6
  1931.8 2.7 convolution_multiply_fusion.3
  1934.5 3.2 constant_dynamic-update-slice_fusion.7
  1937.6 1.8 fusion.115
  1939.5 3.2 constant_dynamic-update-slice_fusion.8
  1944.2 14.5 convolution_convert_fusion.1
  1960.8 20.6 convolution_convert_fusion
  1982.8 5.7 convolution_convert_fusion.3
  1988.5 68.8 %reduce-scatter.7.cloned.1.call-done = f32[128,4096]{0,1:T(8,128)} async-done(((f32[1024,4096]{0,1:T(8,128)}), f32[128,4096]{0,1:T(8,128)}) %reduce-scatter.7.cloned.1.call-update) | async-done | bytes 2097168 | tf_op jit(solution)/shard_map/reduce_scatter | solution.py:242
  2059.6 2.4 copy.134
  2061.9 2.4 copy.135
  2064.3 3.0 add_convert_fusion.1
  2069.7 2.3 pad_maximum_fusion.10
  2072.0 2.0 copy.113
  2074.0 2.1 slice.185
  2076.1 13.2 convolution_convert_fusion.2
  2089.2 22.7 pad_maximum_fusion
  2112.0 11.9 fusion.19
  2124.2 308.3 %reduce-scatter.11.cloned.1.call-done = bf16[1376,2048]{1,0:T(8,128)(2,1)} async-done(((bf16[5504,2048]{1,0:T(8,128)(2,1)}), bf16[1376,2048]{1,0:T(8,128)(2,1)}) %reduce-scatter.11.cloned.1.call-update) | async-done | bytes 5636112 | tf_op jit(solution)/shard_map/reduce_scatter | solution.py:161
  2432.5 740.8 %reduce-scatter.9.cloned.1.call-done = bf16[512,11008]{1,0:T(8,128)(2,1)} async-done(((bf16[2048,11008]{1,0:T(8,128)(2,1)}), bf16[512,11008]{1,0:T(8,128)(2,1)}) %reduce-scatter.9.cloned.1.call-update) | async-done | bytes 11272208 | tf_op jit(solution)/shard_map/reduce_scatter | solution.py:167
  3173.3 556.0 %reduce-scatter.13.cloned.1.call-done = bf16[512,8192]{1,0:T(8,128)(2,1)} async-done(((bf16[2048,8192]{1,0:T(8,128)(2,1)}), bf16[512,8192]{1,0:T(8,128)(2,1)}) %reduce-scatter.13.cloned.1.call-update) | async-done | bytes 8388624
  3731.4 38.0 all-gather.19.cloned.1.call-done
  3769.4 5.0 gather_fusion
  3774.3 2.0 fusion.52
  3776.3 21.7 fusion.36
  3798.0 40.6 all-reduce.1
  3838.6 2.4 fusion.51
  3841.0 245.4 %all-reduce.5.cloned.1.call-done = (bf16[512,8192]{1,0:T(8,128)(2,1)}, bf16[512,11008]{1,0:T(8,128)(2,1)}, bf16[1376,2048]{1,0:T(8,128)(2,1)}) async-done(((bf16[512,8192]{1,0:T(8,128)(2,1)}, bf16[512,11008]{1,0:T(8,128)(2,1)}, bf16[1376,2048]{1,0:T(8,128)(2,1)}), (bf16[512,8192]{1,0:T(8,128)(2,1)}, bf16[512,11008]{1,0:T(8,128)(2,1)}, bf16[1376,2048]{1,0:T(8,128)(2,1)})) %all-reduce.5.cloned.1.call-update) | async-done | bytes 25296912 | tf_op jit(solution)/shard_map/psum | solution.py:268
  4086.3 9.4 slice.157
  4095.7 2.5 slice.158
  4098.3 13.3 convert_element_type.121
  4111.6 5.9 convert_element_type.123
  (284 shorter events, 51.7 us)
Async XLA Ops:
  7.2 430.3 %copy-start.28 = (f32[2048]{0:T(1024)S(1)}, f32[2048]{0:T(1024)}, u32[]{:S(2)}) copy-start(f32[2048]{0:T(1024)} %param.17) | copy-start | bytes 24580
  7.2 430.3 %all-gather.9.cloned.1.call-start = ((), (), s32[]{:S(2)}) async-start(), calls=%async_computation.4 | async-start | bytes 31457280 | tf_op jit(solution)/shard_map/all_gather | solution.py:102
  7.9 466.4 %all-gather.21.cloned.1.call-start = ((), (), s32[]{:S(2)}) async-start(), calls=%async_computation.13 | async-start | bytes 4718592 | tf_op jit(solution)/shard_map/all_gather | solution.py:95
  8.7 522.6 %all-gather.11.cloned.1.call-start = ((), (), s32[]{:S(2)}) async-start(), calls=%async_computation.5 | async-start | bytes 9437184 | tf_op jit(solution)/shard_map/all_gather | solution.py:114
  8.9 1842.4 %copy-start.41 = (pred[128]{0:T(512)(128)(4,1)}, pred[128]{0:T(512)(128)(4,1)S(1)}, u32[]{:S(2)}) copy-start(pred[128]{0:T(512)(128)(4,1)S(1)} %get-tuple-element.344) | copy-start | bytes 388
  9.1 438.9 %copy-start.37 = (f32[128]{0:T(128)}, f32[128]{0:T(128)S(1)}, u32[]{:S(2)}) copy-start(f32[128]{0:T(128)S(1)} %add_rsqrt_fusion.1) | copy-start | bytes 1540
  9.7 439.6 %copy-start.24 = (f32[128,64]{1,0:T(8,128)}, f32[128,64]{1,0:T(8,128)S(1)}, u32[]{:S(2)}) copy-start(f32[128,64]{1,0:T(8,128)S(1)} %get-tuple-element.381) | copy-start | bytes 98308
  9.7 439.6 %copy-start.26 = (f32[128,64]{1,0:T(8,128)}, f32[128,64]{1,0:T(8,128)S(1)}, u32[]{:S(2)}) copy-start(f32[128,64]{1,0:T(8,128)S(1)} %get-tuple-element.382) | copy-start | bytes 98308
  452.1 230.3 %all-gather.13.cloned.1.call-start = ((), (), s32[]{:S(2)}) async-start(), calls=%async_computation.6 | async-start | bytes 10485760 | tf_op jit(solution)/shard_map/all_gather | solution.py:103
  452.6 980.2 %all-gather.15.cloned.1.call-start = ((), (), s32[]{:S(2)}) async-start(), calls=%async_computation.7 | async-start | bytes 56360960 | tf_op jit(solution)/shard_map/all_gather | solution.py:144
  453.2 1361.8 %all-gather.17.cloned.1.call-start = ((), (), s32[]{:S(2)}) async-start(), calls=%async_computation.8 | async-start | bytes 28180480 | tf_op jit(solution)/shard_map/all_gather | solution.py:145
  453.8 1603.5 %reduce-scatter.7.cloned.1.call-start = ((), (), s32[]{:S(2)}) async-start(), calls=%async_computation.10 | async-start | bytes 18874368 | tf_op jit(solution)/shard_map/reduce_scatter | solution.py:242
  453.9 1397.5 %copy-start.44 = (pred[128]{0:T(512)(128)(4,1)}, pred[128]{0:T(512)(128)(4,1)S(1)}, u32[]{:S(2)}) copy-start(pred[128]{0:T(512)(128)(4,1)S(1)} %get-tuple-element.346) | copy-start | bytes 388
  478.5 1372.8 %copy-start.17 = (bf16[128,2048]{1,0:T(8,128)(2,1)}, bf16[128,2048]{1,0:T(8,128)(2,1)S(1)}, u32[]{:S(2)}) copy-start(bf16[128,2048]{1,0:T(8,128)(2,1)S(1)} %gather_fusion.1) | copy-start | bytes 1572868
  536.3 4.9 copy-start
  537.8 4.7 copy-start.2
  546.6 140.5 %copy-start.10 = (bf16[128,16,128]{0,2,1:T(8,128)(2,1)}, bf16[128,16,128]{0,2,1:T(8,128)(2,1)S(1)}, u32[]{:S(2)}) copy-start(bf16[128,16,128]{0,2,1:T(8,128)(2,1)S(1)} %pad_maximum_fusion.9) | copy-start | bytes 1572868
  682.4 750.5 %copy-start.23 = (f32[2048]{0:T(1024)S(1)}, f32[2048]{0:T(1024)}, u32[]{:S(2)}) copy-start(f32[2048]{0:T(1024)} %param.20) | copy-start | bytes 24580
  687.1 1164.2 %copy-start.3 = (f32[128,2048]{1,0:T(8,128)}, f32[128,2048]{1,0:T(8,128)S(1)}, u32[]{:S(2)}) copy-start(f32[128,2048]{1,0:T(8,128)S(1)} %get-tuple-element.392) | copy-start | bytes 3145732
  687.1 1164.2 %copy-start.30 = (f32[128]{0:T(128)}, f32[128]{0:T(128)S(1)}, u32[]{:S(2)}) copy-start(f32[128]{0:T(128)S(1)} %add_rsqrt_fusion) | copy-start | bytes 1540
  1851.8 6.7 copy-start.6
  1867.8 3.4 copy-start.14
  1867.8 3.4 copy-start.1
  1883.1 3.3 copy-start.15
  1883.1 3.3 copy-start.20
  1883.1 3.3 copy-start.33
  1883.1 3.3 copy-start.35
  1883.1 3.3 copy-start.40
  1886.5 3.4 copy-start.14
  1886.6 3.4 copy-start.1
  1902.0 3.3 copy-start.15
  1902.0 3.3 copy-start.20
  1902.0 3.3 copy-start.33
  1902.0 3.3 copy-start.35
  1902.0 3.3 copy-start.40
  1905.3 3.4 copy-start.14
  1905.3 3.4 copy-start.1
  1920.7 3.2 copy-start.33
  1920.7 3.2 copy-start.35
  1920.7 3.3 copy-start.40
  1924.0 3.4 copy-start.14
  1924.1 3.4 copy-start.1
  1939.4 3.3 copy-start.15
  1939.4 3.3 copy-start.20
  1939.4 3.3 copy-start.33
  1939.4 3.3 copy-start.35
  1939.4 3.3 copy-start.40
  1942.8 489.7 %reduce-scatter.11.cloned.1.call-start = ((), (), s32[]{:S(2)}) async-start(), calls=%async_computation.12 | async-start | bytes 28180480 | tf_op jit(solution)/shard_map/reduce_scatter | solution.py:161
  1958.7 1214.6 %reduce-scatter.9.cloned.1.call-start = ((), (), s32[]{:S(2)}) async-start(), calls=%async_computation.11 | async-start | bytes 56360960 | tf_op jit(solution)/shard_map/reduce_scatter | solution.py:167
  1981.4 1747.9 %reduce-scatter.13.cloned.1.call-start = ((), (), s32[]{:S(2)}) async-start(), calls=%async_computation.14 | async-start | bytes 41943040
  2057.3 7.0 copy-start.12
  2057.3 7.0 copy-start.25
  2057.3 7.0 copy-start.27
  2067.3 8.8 copy-start.9
  2067.3 8.8 copy-start.29
  2067.3 8.8 copy-start.38
  2111.9 1657.4 %all-gather.19.cloned.1.call-start = ((), (), s32[]{:S(2)}) async-start(), calls=%async_computation.9 | async-start | bytes 4718592 | tf_op jit(solution)/shard_map/all_gather | solution.py:155
  2123.9 1962.5 %all-reduce.5.cloned.1.call-start = ((), (), s32[]{:S(2)}) async-start(), calls=%async_computation.15 | async-start | bytes 50593792 | tf_op jit(solution)/shard_map/psum | solution.py:268
  3731.3 45.0 %copy-start.21 = (bf16[128,16,128]{0,2,1:T(8,128)(2,1)S(1)}, bf16[128,16,128]{0,2,1:T(8,128)(2,1)}, u32[]{:S(2)}) copy-start(bf16[128,16,128]{0,2,1:T(8,128)(2,1)} %copy.113) | copy-start | bytes 1572868
  3731.4 45.0 %copy-start.22 = (bf16[128,2048]{0,1:T(8,128)(2,1)S(1)}, bf16[128,2048]{0,1:T(8,128)(2,1)}, u32[]{:S(2)}) copy-start(bf16[128,2048]{0,1:T(8,128)(2,1)} %slice.185) | copy-start | bytes 1572868
  3776.3 21.7 copy-start.36
  4086.3 9.4 copy-start.5
  4095.7 15.8 slice-start
  4098.2 13.3 slice-start.1
  (32 other events, 77.7 us)
Sparse Core Ops, SparseCore 0:
  9.6 427.8 all-gather.8
  439.4 34.8 all-gather.20
  476.8 54.3 all-gather.10
  532.7 149.6 all-gather.12
  683.8 748.9 all-gather.14
  1434.2 380.7 all-gather.16
  1942.9 114.3 reduce-scatter.6
  2060.2 372.2 reduce-scatter.10
  2434.9 738.3 reduce-scatter.8
  3175.5 553.7 reduce-scatter.12
  3731.9 37.4 all-gather.18
  3774.0 312.2 all-reduce.4
where the time goes:
time: 4130 us; the launch traced here: 4120 us
  waiting for transfers between devices  3700 us (90%)
  matrix products  201 us (5%)
  local copies, waits for them, and re-layouts  104 us (3%)
  other arithmetic  61.5 us (1%)
    all_gather x1, waiting for transfers between devices, per_device(): lax.all_gather(w_gate_up, 'wa', axis=0, tiled=True)  746 us
    reduce_scatter x1, waiting for transfers between devices, per_device(): lax.psum_scatter(dot_left_t(act_two, d_gate_up_b).astype(jnp.bfloat16), '...  741 us
    unnamed x13, waiting for transfers between devices  559 us
    all_gather x1, waiting for transfers between devices, per_device(): lax.all_gather(w_qkv, 'wa', axis=0, tiled=True)  428 us
    all_gather x1, waiting for transfers between devices, per_device(): lax.all_gather(w_down, 'wa', axis=0, tiled=True)  358 us
    reduce_scatter x1, waiting for transfers between devices, per_device(): lax.psum_scatter(dot_left_t(inner_b, cotangent).astype(jnp.bfloat16), 'wa...  308 us
    psum x1, waiting for transfers between devices, per_device(): lax.psum(attn_share, 'ctx').astype(jnp.float32)  245 us
    all_gather x1, waiting for transfers between devices, per_device(): lax.all_gather(w_out, 'wa', axis=0, tiled=True)  136 us
  transfers between devices with their start and end apart: 12, of which 12 were waited for; matrix products, arithmetic and copies ran while one was open for 5% of the time, Pallas kernels for 0%

commit v1 on v0

--- a/solution.py
+++ b/solution.py
@@ -10,6 +10,17 @@
 WINDOW = 2048
 BLOCK = 128
 EPSILON = 1e-06
+
+
+def collect(x, axis, dim):
+    ways = lax.axis_size(axis)
+    pieces = [x]
+    for far in range(1, ways):
+        pieces.append(
+            lax.ppermute(pieces[far - 1], axis, [(d, (d - 1) % ways) for d in range(ways)])
+        )
+    line = jnp.concatenate(pieces, axis=dim)
+    return jnp.roll(line, lax.axis_index(axis) * x.shape[dim], axis=dim)
 
 
 def dot_plain(left, right):
@@ -98,10 +109,7 @@
     scale_one = rms_scale(inputs)
     normed_one = inputs * scale_one
     act_one = (normed_one * norm1_gain).astype(jnp.bfloat16)
-    full_qkv, full_out = (
-        lax.all_gather(w_qkv, "wa", axis=0, tiled=True),
-        lax.all_gather(w_out, "wa", axis=0, tiled=True),
-    )
+    full_qkv, full_out = (collect(w_qkv, "wa", 0), lax.all_gather(w_out, "wa", axis=0, tiled=True))
     projected = dot_plain(act_one, full_qkv)
     query_b = rotate(projected[:, :width].reshape(tok_rows, HEADS, HEAD), cosine, sine).astype(
         jnp.bfloat16

time: 4130 us -> 4560 us (1.10)
  waiting for transfers between devices: 3700 us -> 4060 us
  local copies, waits for them, and re-layouts: 104 us -> 150 us
    ppermute x0 -> x3, waiting for transfers between devices: none -> 382 us  [collect(): lax.ppermute(pieces[far - 1], axis, [(d, (d - 1) % ways) for d in range(w...]
  transfers between devices with their start and end apart: 12 -> 15, of which waited for: 12 -> 14; matrix products, arithmetic and copies ran while one was open for 5% -> 6% of each run, Pallas kernels for 0% -> 0%
where the time goes in v1:
time: 4560 us; the launch traced here: 4550 us
  waiting for transfers between devices  4060 us (89%)
  matrix products  203 us (4%)
  local copies, waits for them, and re-layouts  150 us (3%)
  other arithmetic  64.9 us (1%)
    all_gather x1, waiting for transfers between devices, per_device(): lax.all_gather(w_gate_up, 'wa', axis=0, tiled=True)  746 us
    reduce_scatter x1, waiting for transfers between devices, per_device(): lax.psum_scatter(dot_left_t(act_two, d_gate_up_b).astype(jnp.bfloat16), '...  741 us
    unnamed x13, waiting for transfers between devices  558 us
    all_gather x1, waiting for transfers between devices, per_device(): lax.all_gather(w_qkv, 'wa', axis=0, tiled=True)  420 us
    ppermute x3, waiting for transfers between devices, collect(): lax.ppermute(pieces[far - 1], axis, [(d, (d - 1) % ways) for d in range(w...  382 us
    all_gather x1, waiting for transfers between devices, per_device(): lax.all_gather(w_down, 'wa', axis=0, tiled=True)  358 us
    reduce_scatter x1, waiting for transfers between devices, per_device(): lax.psum_scatter(dot_left_t(inner_b, cotangent).astype(jnp.bfloat16), 'wa...  307 us
    psum x1, waiting for transfers between devices, per_device(): lax.psum(attn_share, 'ctx').astype(jnp.float32)  252 us
  transfers between devices with their start and end apart: 15, of which 14 were waited for; matrix products, arithmetic and copies ran while one was open for 6% of the time, Pallas kernels for 0%

profile of v1, /device:TPU:0, one launch (start us, length us, event | category | flops | bytes accessed | tf_op | source)
XLA Modules:
  0.0 4546.0 jit_solution(18290365159471502219)
XLA Ops:
  7.2 5.1 collective-permute-start
  12.3 135.1 %collective-permute-done = bf16[512,6144]{1,0:T(8,128)(2,1)S(1)} collective-permute-done((bf16[512,6144]{1,0:T(8,128)(2,1)}, bf16[512,6144]{1,0:T(8,128)(2,1)S(1)}, u32[]{:S(2)}, u32[]{:S(2)}) %collective-permute-start) | collective-permute-done | bytes 6291488 | tf_op jit(solution)/shard_map/ppermute | solution.py:20
  147.4 2.7 copy-done.6
  150.1 4.2 collective-permute-start.1
  154.3 133.9 %collective-permute-done.1 = bf16[512,6144]{1,0:T(8,128)(2,1)} collective-permute-done((bf16[512,6144]{1,0:T(8,128)(2,1)S(1)}, bf16[512,6144]{1,0:T(8,128)(2,1)}, u32[]{:S(2)}, u32[]{:S(2)}) %collective-permute-start.1) | collective-permute-done | bytes 6291488 | tf_op jit(solution)/shard_map/ppermute | solution.py:20
  288.2 4.4 collective-permute-start.2
  296.5 6.9 constant_dynamic-update-slice_fusion.10
  303.4 3.1 constant_dynamic-update-slice_fusion.9
  306.5 6.3 constant_dynamic-update-slice_fusion.8
  312.8 113.1 %collective-permute-done.2 = bf16[512,6144]{1,0:T(8,128)(2,1)} collective-permute-done((bf16[512,6144]{1,0:T(8,128)(2,1)}, bf16[512,6144]{1,0:T(8,128)(2,1)}, u32[]{:S(2)}, u32[]{:S(2)}) %collective-permute-start.2) | collective-permute-done | bytes 6291488 | tf_op jit(solution)/shard_map/ppermute | solution.py:20
  425.9 6.2 constant_dynamic-update-slice_fusion.7
  432.1 3.1 constant_dynamic-update-slice_fusion.6
  435.2 3.1 constant_dynamic-update-slice_fusion.5
  438.3 6.1 constant_dynamic-update-slice_fusion.4
  444.5 6.2 constant_dynamic-update-slice_fusion.3
  450.7 13.4 fusion.18
  473.4 4.2 gather_fusion.1
  477.9 49.5 %all-gather.9.cloned.1.call-done = bf16[1024,4096]{1,0:T(8,128)(2,1)} async-done(((bf16[128,4096]{1,0:T(8,128)(2,1)}), bf16[1024,4096]{1,0:T(8,128)(2,1)}) %all-gather.9.cloned.1.call-update) | async-done | bytes 8388624 | tf_op jit(solution)/shard_map/all_gather | solution.py:122
  527.4 3.8 slice_bitcast_fusion.1
  542.6 136.0 %all-gather.11.cloned.1.call-done = bf16[2048,2048]{1,0:T(8,128)(2,1)} async-done(((bf16[512,2048]{1,0:T(8,128)(2,1)}), bf16[2048,2048]{1,0:T(8,128)(2,1)}) %all-gather.11.cloned.1.call-update) | async-done | bytes 8388624 | tf_op jit(solution)/shard_map/all_gather | solution.py:112
  678.6 4.8 multiply_reduce_fusion.3
  683.4 745.7 %all-gather.13.cloned.1.call-done = bf16[2048,11008]{1,0:T(8,128)(2,1)} async-done(((bf16[512,11008]{1,0:T(8,128)(2,1)}), bf16[2048,11008]{1,0:T(8,128)(2,1)}) %all-gather.13.cloned.1.call-update) | async-done | bytes 45088784 | tf_op jit(solution)/shard_map/all_gather | solution.py:152
  1429.1 24.1 fusion.66
  1453.2 358.1 %all-gather.15.cloned.1.call-done = bf16[5504,2048]{1,0:T(8,128)(2,1)} async-done(((bf16[1376,2048]{1,0:T(8,128)(2,1)}), bf16[5504,2048]{1,0:T(8,128)(2,1)}) %all-gather.15.cloned.1.call-update) | async-done | bytes 22544400 | tf_op jit(solution)/shard_map/all_gather | solution.py:153
  1811.3 14.9 multiply_convert_fusion.2
  1826.1 21.4 multiply_reduce_fusion.1
  1848.0 6.7 fusion.27
  1855.8 7.9 broadcast_in_dim.154
  1863.7 75.1 %while.18 = (s32[]{:T(128)}, f32[128,16,128]{2,0,1:T(8,128)}, f32[1024,4096]{0,1:T(8,128)}, bf16[1024,16,128]{2,0,1:T(8,128)(2,1)}, bf16[128,16,128]{2,0,1:T(8,1...) while((s32[]{:T(128)}, f32[128,16,128]{2,0,1:T(8,128)}, ...), condition=%wide.region_14.16_spmd.clone, body=%wide.region_12.15_spmd.clone.sunk | while | flops 677182976 | bytes 61174424 | solution.py:247
  1863.9 2.5 constant_dynamic-slice_fusion.6
  1871.6 2.7 convolution_multiply_fusion.3
  1874.3 3.2 constant_dynamic-update-slice_fusion.15
  1879.3 3.2 constant_dynamic-update-slice_fusion.16
  1882.7 2.5 constant_dynamic-slice_fusion.6
  1890.3 2.7 convolution_multiply_fusion.3
  1893.0 3.1 constant_dynamic-update-slice_fusion.15
  1898.0 3.2 constant_dynamic-update-slice_fusion.16
  1909.0 2.7 convolution_multiply_fusion.3
  1911.8 3.1 constant_dynamic-update-slice_fusion.15
  1916.7 3.3 constant_dynamic-update-slice_fusion.16
  1927.8 2.7 convolution_multiply_fusion.3
  1930.5 3.2 constant_dynamic-update-slice_fusion.15
  1935.5 3.2 constant_dynamic-update-slice_fusion.16
  1940.3 14.5 convolution_convert_fusion.1
  1956.8 20.6 convolution_convert_fusion
  1978.8 5.7 convolution_convert_fusion.3
  1984.6 68.8 %reduce-scatter.7.cloned.1.call-done = f32[128,4096]{0,1:T(8,128)} async-done(((f32[1024,4096]{0,1:T(8,128)}), f32[128,4096]{0,1:T(8,128)}) %reduce-scatter.7.cloned.1.call-update) | async-done | bytes 2097168 | tf_op jit(solution)/shard_map/reduce_scatter | solution.py:250
  2060.5 3.0 add_convert_fusion.1
  2072.3 13.1 convolution_convert_fusion.2
  2085.4 23.2 pad_maximum_fusion
  2108.6 11.8 fusion.21
  2121.3 307.3 %reduce-scatter.11.cloned.1.call-done = bf16[1376,2048]{1,0:T(8,128)(2,1)} async-done(((bf16[5504,2048]{1,0:T(8,128)(2,1)}), bf16[1376,2048]{1,0:T(8,128)(2,1)}) %reduce-scatter.11.cloned.1.call-update) | async-done | bytes 5636112 | tf_op jit(solution)/shard_map/reduce_scatter | solution.py:169
  2428.6 740.8 %reduce-scatter.9.cloned.1.call-done = bf16[512,11008]{1,0:T(8,128)(2,1)} async-done(((bf16[2048,11008]{1,0:T(8,128)(2,1)}), bf16[512,11008]{1,0:T(8,128)(2,1)}) %reduce-scatter.9.cloned.1.call-update) | async-done | bytes 11272208 | tf_op jit(solution)/shard_map/reduce_scatter | solution.py:175
  3169.4 556.1 %reduce-scatter.13.cloned.1.call-done = bf16[512,8192]{1,0:T(8,128)(2,1)} async-done(((bf16[2048,8192]{1,0:T(8,128)(2,1)}), bf16[512,8192]{1,0:T(8,128)(2,1)}) %reduce-scatter.13.cloned.1.call-update) | async-done | bytes 8388624
  3727.6 37.9 all-gather.17.cloned.1.call-done
  3765.5 5.0 gather_fusion
  3772.4 419.9 %all-gather.19.cloned.1.call-done = bf16[2048,6144]{1,0:T(8,128)(2,1)} async-done(((bf16[512,6144]{1,0:T(8,128)(2,1)}), bf16[2048,6144]{1,0:T(8,128)(2,1)}) %all-gather.19.cloned.1.call-update) | async-done | bytes 25165840 | tf_op jit(solution)/shard_map/all_gather | solution.py:186
  4192.3 20.5 fusion.38
  4212.9 40.3 all-reduce.1
  4255.5 252.0 %all-reduce.5.cloned.1.call-done = (bf16[512,8192]{1,0:T(8,128)(2,1)}, bf16[512,11008]{1,0:T(8,128)(2,1)}, bf16[1376,2048]{1,0:T(8,128)(2,1)}) async-done(((bf16[512,8192]{1,0:T(8,128)(2,1)}, bf16[512,11008]{1,0:T(8,128)(2,1)}, bf16[1376,2048]{1,0:T(8,128)(2,1)}), (bf16[512,8192]{1,0:T(8,128)(2,1)}, bf16[512,11008]{1,0:T(8,128)(2,1)}, bf16[1376,2048]{1,0:T(8,128)(2,1)})) %all-reduce.5.cloned.1.call-update) | async-done | bytes 25296912 | tf_op jit(solution)/shard_map/psum | solution.py:276
  4507.5 9.4 slice.157
  4516.9 2.5 slice.158
  4519.4 13.3 convert_element_type.121
  4532.7 5.9 convert_element_type.123
  (305 shorter events, 86.2 us)
Async XLA Ops:
  7.2 466.2 %all-gather.21.cloned.1.call-start = ((), (), s32[]{:S(2)}) async-start(), calls=%async_computation.13 | async-start | bytes 4718592 | tf_op jit(solution)/shard_map/all_gather | solution.py:106
  7.2 140.2 %collective-permute-start = (bf16[512,6144]{1,0:T(8,128)(2,1)}, bf16[512,6144]{1,0:T(8,128)(2,1)S(1)}, u32[]{:S(2)}, u32[]{:S(2)}) collective-permute-start(bf16[512,6144]{1,0:T(8,128)(2,1)} %param.18), channel_id=1, source_target_pairs={{0,3},{1,0},{2,1},{3,2},{4,7},{5,4},{6,5},{7,6},{8,11},{9,8},{10,9... | collective-permute-start | bytes 18874376 | tf_op jit(solution)/shard_map/ppermute | solution.py:20
  150.1 138.1 %collective-permute-start.1 = (bf16[512,6144]{1,0:T(8,128)(2,1)S(1)}, bf16[512,6144]{1,0:T(8,128)(2,1)}, u32[]{:S(2)}, u32[]{:S(2)}) collective-permute-start(bf16[512,6144]{1,0:T(8,128)(2,1)S(1)} %collective-permute-done), channel_id=1, source_target_pairs={{0,3},{1,0},{2,1},{3,2},{4,7},{5,4},{6,5},{7,6},{8,11},{9,8},{10,9... | collective-permute-start | bytes 18874376 | tf_op jit(solution)/shard_map/ppermute | solution.py:20
  288.2 137.7 %collective-permute-start.2 = (bf16[512,6144]{1,0:T(8,128)(2,1)}, bf16[512,6144]{1,0:T(8,128)(2,1)}, u32[]{:S(2)}, u32[]{:S(2)}) collective-permute-start(bf16[512,6144]{1,0:T(8,128)(2,1)} %collective-permute-done.1), channel_id=1, source_target_pairs={{0,3},{1,0},{2,1},{3,2},{4,7},{5,4},{6,5},{7,6},{8,11},{9,8},{10,9... | collective-permute-start | bytes 18874376 | tf_op jit(solution)/shard_map/ppermute | solution.py:20
  292.6 234.8 %all-gather.9.cloned.1.call-start = ((), (), s32[]{:S(2)}) async-start(), calls=%async_computation.4 | async-start | bytes 9437184 | tf_op jit(solution)/shard_map/all_gather | solution.py:122
  293.5 1554.0 %copy-start.42 = (pred[128]{0:T(512)(128)(4,1)}, pred[128]{0:T(512)(128)(4,1)S(1)}, u32[]{:S(2)}) copy-start(pred[128]{0:T(512)(128)(4,1)S(1)} %get-tuple-element.344) | copy-start | bytes 388
  294.7 156.0 %copy-start.40 = (f32[128]{0:T(128)}, f32[128]{0:T(128)S(1)}, u32[]{:S(2)}) copy-start(f32[128]{0:T(128)S(1)} %add_rsqrt_fusion.1) | copy-start | bytes 1540
  296.2 7.2 slice-start.2
  296.5 171.7 %copy-start.25 = (f32[128,64]{1,0:T(8,128)}, f32[128,64]{1,0:T(8,128)S(1)}, u32[]{:S(2)}) copy-start(f32[128,64]{1,0:T(8,128)S(1)} %get-tuple-element.381) | copy-start | bytes 98308
  296.5 171.7 %copy-start.27 = (f32[128,64]{1,0:T(8,128)}, f32[128,64]{1,0:T(8,128)S(1)}, u32[]{:S(2)}) copy-start(f32[128,64]{1,0:T(8,128)S(1)} %get-tuple-element.382) | copy-start | bytes 98308
  296.5 6.9 slice-start.3
  306.5 125.6 %slice-start = ((s8[6291456]{0:T(1024)(128)(4,1)}), s8[4194304]{0:T(1024)(128)(4,1)S(1)}, s32[]{:S(2)}) async-start(s8[6291456]{0:T(1024)(128)(4,1)} %bitcast.96), calls=%async_computation.16 | async-start | bytes 8388608
  312.8 119.3 %slice-start.1 = ((s8[6291456]{0:T(1024)(128)(4,1)}), s8[2097152]{0:T(1024)(128)(4,1)S(1)}, s32[]{:S(2)}) async-start(s8[6291456]{0:T(1024)(128)(4,1)} %bitcast.96), calls=%async_computation.17 | async-start | bytes 4194304
  444.5 6.2 copy-start.11
  444.5 6.3 copy-start.29
  470.9 207.7 %all-gather.11.cloned.1.call-start = ((), (), s32[]{:S(2)}) async-start(), calls=%async_computation.5 | async-start | bytes 10485760 | tf_op jit(solution)/shard_map/all_gather | solution.py:112
  471.6 957.4 %all-gather.13.cloned.1.call-start = ((), (), s32[]{:S(2)}) async-start(), calls=%async_computation.6 | async-start | bytes 56360960 | tf_op jit(solution)/shard_map/all_gather | solution.py:152
  472.2 1339.0 %all-gather.15.cloned.1.call-start = ((), (), s32[]{:S(2)}) async-start(), calls=%async_computation.7 | async-start | bytes 28180480 | tf_op jit(solution)/shard_map/all_gather | solution.py:153
  472.8 1580.6 %reduce-scatter.7.cloned.1.call-start = ((), (), s32[]{:S(2)}) async-start(), calls=%async_computation.9 | async-start | bytes 18874368 | tf_op jit(solution)/shard_map/reduce_scatter | solution.py:250
  473.1 1374.5 %copy-start.44 = (pred[128]{0:T(512)(128)(4,1)}, pred[128]{0:T(512)(128)(4,1)S(1)}, u32[]{:S(2)}) copy-start(pred[128]{0:T(512)(128)(4,1)S(1)} %get-tuple-element.346) | copy-start | bytes 388
  477.6 1370.0 %copy-start.18 = (bf16[128,2048]{1,0:T(8,128)(2,1)}, bf16[128,2048]{1,0:T(8,128)(2,1)S(1)}, u32[]{:S(2)}) copy-start(bf16[128,2048]{1,0:T(8,128)(2,1)S(1)} %gather_fusion.1) | copy-start | bytes 1572868
  532.3 4.9 copy-start
  533.7 4.7 copy-start.2
  542.6 140.8 %copy-start.9 = (bf16[128,16,128]{0,2,1:T(8,128)(2,1)}, bf16[128,16,128]{0,2,1:T(8,128)(2,1)S(1)}, u32[]{:S(2)}) copy-start(bf16[128,16,128]{0,2,1:T(8,128)(2,1)S(1)} %pad_maximum_fusion.9) | copy-start | bytes 1572868
  678.6 750.5 %copy-start.24 = (f32[2048]{0:T(1024)S(1)}, f32[2048]{0:T(1024)}, u32[]{:S(2)}) copy-start(f32[2048]{0:T(1024)} %param.20) | copy-start | bytes 24580
  683.4 1164.2 %copy-start.3 = (f32[128,2048]{1,0:T(8,128)}, f32[128,2048]{1,0:T(8,128)S(1)}, u32[]{:S(2)}) copy-start(f32[128,2048]{1,0:T(8,128)S(1)} %get-tuple-element.392) | copy-start | bytes 3145732
  683.4 1164.2 %copy-start.31 = (f32[128]{0:T(128)}, f32[128]{0:T(128)S(1)}, u32[]{:S(2)}) copy-start(f32[128]{0:T(128)S(1)} %add_rsqrt_fusion) | copy-start | bytes 1540
  1848.0 6.7 copy-start.7
  1863.9 4.4 copy-start.15
  1863.9 4.4 copy-start.33
  1863.9 4.4 copy-start.38
  1863.9 3.4 copy-start.1
  1882.6 4.4 copy-start.15
  1882.6 4.4 copy-start.33
  1882.6 4.4 copy-start.38
  1882.7 3.4 copy-start.1
  1901.3 4.4 copy-start.15
  1901.3 4.4 copy-start.33
  1901.3 4.4 copy-start.38
  1901.4 3.4 copy-start.1
  1916.7 3.3 copy-start.36
  1916.7 3.3 copy-start.39
  1920.1 4.4 copy-start.15
  1920.1 4.4 copy-start.33
  1920.1 4.4 copy-start.38
  1920.1 3.4 copy-start.1
  1938.9 489.7 %reduce-scatter.11.cloned.1.call-start = ((), (), s32[]{:S(2)}) async-start(), calls=%async_computation.12 | async-start | bytes 28180480 | tf_op jit(solution)/shard_map/reduce_scatter | solution.py:169
  1954.8 1214.6 %reduce-scatter.9.cloned.1.call-start = ((), (), s32[]{:S(2)}) async-start(), calls=%async_computation.11 | async-start | bytes 56360960 | tf_op jit(solution)/shard_map/reduce_scatter | solution.py:175
  1977.5 1748.0 %reduce-scatter.13.cloned.1.call-start = ((), (), s32[]{:S(2)}) async-start(), calls=%async_computation.14 | async-start | bytes 41943040
  2054.7 5.8 copy-start.13
  2054.7 5.8 copy-start.26
  2054.7 5.8 copy-start.28
  2063.4 8.8 copy-start.12
  2063.4 8.8 copy-start.30
  2063.4 8.8 copy-start.41
  2108.6 1656.9 %all-gather.17.cloned.1.call-start = ((), (), s32[]{:S(2)}) async-start(), calls=%async_computation.8 | async-start | bytes 4718592 | tf_op jit(solution)/shard_map/all_gather | solution.py:163
  2120.5 2071.8 %all-gather.19.cloned.1.call-start = ((), (), s32[]{:S(2)}) async-start(), calls=%async_computation.10 | async-start | bytes 31457280 | tf_op jit(solution)/shard_map/all_gather | solution.py:186
  2121.2 2386.2 %all-reduce.5.cloned.1.call-start = ((), (), s32[]{:S(2)}) async-start(), calls=%async_computation.15 | async-start | bytes 50593792 | tf_op jit(solution)/shard_map/psum | solution.py:276
  3725.5 466.8 %copy-start.22 = (bf16[128,16,128]{0,2,1:T(8,128)(2,1)S(1)}, bf16[128,16,128]{0,2,1:T(8,128)(2,1)}, u32[]{:S(2)}) copy-start(bf16[128,16,128]{0,2,1:T(8,128)(2,1)} %copy.113) | copy-start | bytes 1572868
  3725.6 466.8 %copy-start.23 = (bf16[128,2048]{0,1:T(8,128)(2,1)S(1)}, bf16[128,2048]{0,1:T(8,128)(2,1)}, u32[]{:S(2)}) copy-start(bf16[128,2048]{0,1:T(8,128)(2,1)} %slice.185) | copy-start | bytes 1572868
  3772.4 440.5 %copy-start.37 = (f32[2048]{0:T(1024)S(1)}, f32[2048]{0:T(1024)}, u32[]{:S(2)}) copy-start(f32[2048]{0:T(1024)} %get-tuple-element.311) | copy-start | bytes 24580
  4507.5 9.4 copy-start.5
  4516.9 15.8 slice-start.4
  4519.4 13.3 slice-start.5
  (37 other events, 101.2 us)
Sparse Core Ops, SparseCore 0:
  292.7 34.9 all-gather.20
  471.0 56.3 all-gather.8
  528.9 149.6 all-gather.10
  680.1 748.9 all-gather.12
  1430.5 380.7 all-gather.14
  1939.0 114.3 reduce-scatter.6
  2056.3 372.2 reduce-scatter.10
  2431.0 738.3 reduce-scatter.8
  3171.7 553.7 reduce-scatter.12
  3728.0 37.4 all-gather.16
  3767.1 425.1 all-gather.18
  4197.0 310.4 all-reduce.4
